TPU v7x, 32 devices: a whole 2x2x4 slice. The times are simulated.
32 devices in a mesh: row: 8 (over z, y), col: 4 (over x, core).
Axes of the slice: x: 2, y: 2, z: 4, core: 2. Of those that a mesh axis runs over, the one named last changes fastest.
Arguments:
- rhs: float32 [32768, 256], P(('row', 'col')), may hold values from -6 to 6
- local_mat: bfloat16 [32768, 1024], P(('row', 'col')), may hold values from -1 to 5
- local_inv: bfloat16 [32768, 1024], P(('row', 'col')), may hold values from -1 to 1
- basis_t: bfloat16 [3072, 1024], P(('row', 'col')), may hold values from -0.1875 to 0.1875
- coarse_inv: bfloat16 [3072, 3072], P('col', 'row'), may hold values from -0.109375 to 0.109375
- couple: float32 [32, 4, 128], P(('row', 'col')), may hold values from 0.5 to 2
- margin_rows: int32 [32, 4, 128], P(('row', 'col')), may hold values from 0 to 1023, as said below
Outputs:
- solution: float32 [32768, 256], P(('row', 'col'))
- residual: float32 [32768, 256], P(('row', 'col'))
Inputs may be any that keep to these rules, and one draw needn't show every extreme that they name: `margin_rows`: within each subdomain the 512 listed rows are all different.
All inputs are finite; a program needn't handle non-finite values.
Results may differ from a plain program's by a relative error of at most 0.024.
Values may be sent and summed in bfloat16 or wider, within the bound.
No kernel may reach another device: no remote copies, remote signals or barrier semaphores. Data moves between devices by JAX's collectives and lax.ppermute only.
A program may use at most 64 MiB of HBM per device.

v0:
```python
import jax
import jax.numpy as jnp
from jax import lax
from jax.sharding import PartitionSpec as P

STEPS = 2


def padded(cells, sides, width):
    for axis, dim in sides:
        count = lax.axis_size(axis)
        ends = count - 1
        head = lax.slice_in_dim(cells, 0, width, axis=dim)
        tail = lax.slice_in_dim(cells, cells.shape[dim] - width, cells.shape[dim], axis=dim)
        cells = jnp.concatenate(
            [
                lax.ppermute(tail, axis, [(i, (i + 1) % count) for i in range(ends)]),
                cells,
                lax.ppermute(head, axis, [((i + 1) % count, i) for i in range(ends)]),
            ],
            axis=dim,
        )
    return cells


def per_device(rhs, local_mat, local_inv, basis_t, coarse_inv, couple, margin_rows):
    face_index = margin_rows[0]
    flat_rows = face_index.reshape(-1)
    weights = couple[0]
    columns = rhs.shape[1]

    def neighbour_faces(vector_b):
        face_vals = vector_b[face_index]
        north_south = padded(face_vals[0:2], (("row", 0),), 1)
        west_east = padded(face_vals[2:4], (("col", 0),), 1)
        received = jnp.stack([north_south[0], north_south[3], west_east[0], west_east[3]])
        return received

    def apply_operator(vector):
        vector_b = vector.astype(jnp.bfloat16)
        received = neighbour_faces(vector_b)
        coupling_terms = (weights[:, :, None] * received.astype(jnp.float32)).reshape(-1, columns)
        coupled = jnp.zeros(vector.shape, jnp.float32).at[flat_rows].add(coupling_terms)
        return jnp.dot(local_mat, vector_b, preferred_element_type=jnp.float32) - coupled

    solution = jnp.zeros(rhs.shape, jnp.float32)
    residual = rhs
    for sweep in range(STEPS):
        if sweep > 0:
            residual = rhs - apply_operator(solution)
        rounded = residual.astype(jnp.bfloat16)
        restricted = jnp.dot(basis_t, rounded, preferred_element_type=jnp.float32).astype(
            jnp.bfloat16
        )
        block_rows = restricted.shape[0]
        partial_sum = jnp.dot(
            coarse_inv,
            lax.all_gather(restricted, "col", axis=0, tiled=True),
            preferred_element_type=jnp.float32,
        )
        summed = lax.psum(partial_sum, "row")
        coarse_part = lax.dynamic_slice_in_dim(
            summed, lax.axis_index("row") * block_rows, block_rows, 0
        )
        coarse_b = coarse_part.astype(jnp.bfloat16)
        solution = solution + lax.dot_general(
            basis_t, coarse_b, (((0,), (0,)), ((), ())), preferred_element_type=jnp.float32
        )
        residual = rhs - apply_operator(solution)
        solution = solution + jnp.dot(
            local_inv, residual.astype(jnp.bfloat16), preferred_element_type=jnp.float32
        )
    residual = rhs - apply_operator(solution)
    return (solution, residual)


def solution(mesh):
    placed = (
        P(("row", "col"), None),
        P(("row", "col"), None),
        P(("row", "col"), None),
        P(("row", "col"), None),
        P("col", "row"),
        P(("row", "col"), None, None),
        P(("row", "col"), None, None),
    )
    return jax.shard_map(
        per_device,
        mesh=mesh,
        in_specs=placed,
        out_specs=(P(("row", "col"), None), P(("row", "col"), None)),
        check_vma=False,
    )
```

profile of v0, /device:TPU:9, one launch (start us, length us, event | category | flops | bytes accessed | tf_op | source)
XLA Modules:
  0.0 242.6 jit_solution(8589869174017089495)
XLA Ops:
  0.7 0.8 fusion.35
  1.5 1.6 convolution_convert_fusion
  3.1 6.1 %all_gather.6 = bf16[384,256]{1,0:T(8,128)(2,1)S(1)} all-gather(bf16[96,256]{1,0:T(8,128)(2,1)S(1)} %convolution_convert_fusion), channel_id=1, replica_groups=mesh['row'=8,'col'=4] {'col'}, dimensions={0}, use_global_device_ids=true | all-gather | bytes 245760 | tf_op jit(solution)/shard_map/all_gather | solution.py:58
  9.2 1.5 convolution_bitcast_fusion.5
  10.7 40.2 %all-reduce.2 = bf16[768,256]{0,1:T(8,128)(2,1)} all-reduce(f32[768,256]{0,1:T(8,128)S(1)} %convolution_bitcast_fusion.5), channel_id=1, replica_groups=mesh['row'=8,'col'=4] {'row'}, use_global_device_ids=true, to_apply=%region_0.0 | all-reduce | flops 196608 | bytes 1179648 | tf_op jit(solution)/shard_map/psum | solution.py:61
  50.8 1.2 fusion.34
  52.1 1.0 copy-done.2
  53.1 0.2 copy.31
  53.4 2.0 gather_fusion
  55.3 0.7 slice_bitcast_fusion.15
  56.0 1.9 collective-permute-start
  57.9 8.7 %collective-permute-start.2 = (bf16[1,128,256]{2,1,0:T(8,128)(2,1)}, bf16[1,128,256]{2,1,0:T(8,128)(2,1)}, u32[]{:S(2)}, u32[]{:S(2)}) collective-permute-start(bf16[1,128,256]{2,1,0:T(8,128)(2,1)} %get-tuple-element.21), channel_id=1, source_target_pairs={{0,1},{1,2},{2,3},{4,5},{5,6},{6,7},{8,9},{9,10},{10,11},{12,13},{... | collective-permute-start | bytes 196616 | tf_op jit(solution)/shard_map/ppermute | solution.py:17
  66.6 3.3 %collective-permute-start.1 = (bf16[1,128,256]{2,1,0:T(8,128)(2,1)S(1)}, bf16[1,128,256]{2,1,0:T(8,128)(2,1)}, u32[]{:S(2)}, u32[]{:S(2)}) collective-permute-start(bf16[1,128,256]{2,1,0:T(8,128)(2,1)S(1)} %get-tuple-element.22), channel_id=1, source_target_pairs={{4,0},{8,4},{12,8},{16,12},{20,16},{24,20},{28,24},{5,1},{9,5},{13... | collective-permute-start | bytes 196616 | tf_op jit(solution)/shard_map/ppermute | solution.py:19
  69.9 1.9 collective-permute-start.3
  71.9 1.6 copy.33
  73.5 2.1 collective-permute-done.3
  75.6 1.6 pad_maximum_fusion
  77.3 4.8 %scatter_custom_fusion = f32[1024,256]{1,0:T(8,128)} fusion(s32[512]{0:T(512)S(1)} %bitcast.127, bf16[512,256]{1,0:T(8,128)(2,1)} %bitcast.119, f32[]{:T(128)} %constant.4.clone.1, f32[512]{0:T(512)S(1)} %bitcast.122), kind=kCustom, calls=%fused_computation.40 | custom fusion | flops 393216 | bytes 1312772 | tf_op jit(solution)/shard_map/scatter-add | solution.py:43
  82.1 2.5 %copy.32 = f32[1024,256]{0,1:T(8,128)} copy(f32[1024,256]{1,0:T(8,128)} %scatter_custom_fusion) | data formatting | bytes 2097152 | tf_op jit(solution)/shard_map/scatter-add | solution.py:43
  84.6 4.8 %convolution_add_fusion.2 = f32[256,1024]{1,0:T(8,128)} fusion(f32[256,1024]{1,0:T(8,128)} %copy-done.2, bf16[1024,1024]{1,0:T(8,128)(2,1)} %param.9, f32[1024,256]{0,1:T(8,128)S(1)} %copy.33, f32[1024,256]{0,1:T(8,128)} %copy.32, bf16[1024,1024]{1,0:T(8,128)(2,1)S(1)} %copy-done), kind=kOutput, calls=%fused_computation.23 | convolution fusion | flops 1075052544 | bytes 8388608 | tf_op jit(solution)/shard_map/dot_general | solution.py:70
  89.4 2.1 convert_bitcast_fusion.1
  91.5 2.0 copy.34
  93.5 3.3 %gather_fusion.1 = bf16[512,256]{1,0:T(8,128)(2,1)} fusion(bf16[1024,256]{1,0:T(8,128)(2,1)} %copy.34, s32[1024]{0:T(1024)S(1)} %pad_clamp_fusion), kind=kCustom, calls=%fused_computation.1 | custom fusion | bytes 526336 | tf_op jit(solution)/shard_map/gather | solution.py:33
  96.8 1.0 slice_bitcast_fusion.11
  97.8 1.9 collective-permute-start.4
  99.7 2.0 collective-permute-start.6
  101.8 4.2 %collective-permute-start.5 = (bf16[1,128,256]{2,1,0:T(8,128)(2,1)S(1)}, bf16[1,128,256]{2,1,0:T(8,128)(2,1)S(1)}, u32[]{:S(2)}, u32[]{:S(2)}) collective-permute-start(bf16[1,128,256]{2,1,0:T(8,128)(2,1)S(1)} %get-tuple-element.18), channel_id=1, source_target_pairs={{4,0},{8,4},{12,8},{16,12},{20,16},{24,20},{28,24},{5,1},{9,5},{13... | collective-permute-start | bytes 196616 | tf_op jit(solution)/shard_map/ppermute | solution.py:19
  106.0 2.6 %collective-permute-start.7 = (bf16[1,128,256]{2,1,0:T(8,128)(2,1)S(1)}, bf16[1,128,256]{2,1,0:T(8,128)(2,1)S(1)}, u32[]{:S(2)}, u32[]{:S(2)}) collective-permute-start(bf16[1,128,256]{2,1,0:T(8,128)(2,1)S(1)} %get-tuple-element.19), channel_id=1, source_target_pairs={{1,0},{2,1},{3,2},{5,4},{6,5},{7,6},{9,8},{10,9},{11,10},{13,12},{... | collective-permute-start | bytes 196616 | tf_op jit(solution)/shard_map/ppermute | solution.py:19
  108.6 3.0 %collective-permute-done.7 = bf16[1,128,256]{2,1,0:T(8,128)(2,1)S(1)} collective-permute-done((bf16[1,128,256]{2,1,0:T(8,128)(2,1)S(1)}, bf16[1,128,256]{2,1,0:T(8,128)(2,1)S(1)}, u32[]{:S(2)}, u32[]{:S(2)}) %collective-permute-start.7) | collective-permute-done | bytes 65568 | tf_op jit(solution)/shard_map/ppermute | solution.py:19
  111.6 0.7 pad_maximum_fusion.1
  112.3 4.8 %scatter_custom_fusion.1 = f32[1024,256]{1,0:T(8,128)} fusion(s32[512]{0:T(512)S(1)} %bitcast.128, bf16[512,256]{1,0:T(8,128)(2,1)} %bitcast.120, f32[]{:T(128)} %constant.4.clone.1, f32[512]{0:T(512)S(1)} %bitcast.123), kind=kCustom, calls=%fused_computation.38 | custom fusion | flops 393216 | bytes 1312772 | tf_op jit(solution)/shard_map/scatter-add | solution.py:43
  117.1 2.5 %copy.35 = f32[1024,256]{0,1:T(8,128)} copy(f32[1024,256]{1,0:T(8,128)} %scatter_custom_fusion.1) | data formatting | bytes 2097152 | tf_op jit(solution)/shard_map/scatter-add | solution.py:43
  119.7 2.5 %fusion.14 = bf16[96,256]{1,0:T(8,128)(2,1)S(1)} fusion(bf16[96,1024]{1,0:T(8,128)(2,1)S(1)} %copy-done.3, f32[1024,256]{0,1:T(8,128)S(1)} %copy.33, f32[1024,256]{0,1:T(8,128)} %copy.35, bf16[1024,1024]{1,0:T(8,128)(2,1)S(1)} %copy-done, f32[256,1024]{1,0:T(8,128)} %convolution_add_fusion.2), kind=kOutput, calls=%fused_computation.32 | convolution fusion | flops 588275712 | bytes 5488640 | tf_op jit(solution)/shard_map/dot_general | solution.py:52
  122.2 4.4 %all_gather.7 = bf16[384,256]{1,0:T(8,128)(2,1)S(1)} all-gather(bf16[96,256]{1,0:T(8,128)(2,1)S(1)} %fusion.14), channel_id=1, replica_groups=mesh['row'=8,'col'=4] {'col'}, dimensions={0}, use_global_device_ids=true | all-gather | bytes 245760 | tf_op jit(solution)/shard_map/all_gather | solution.py:58
  126.6 2.4 convolution_bitcast_fusion.4
  129.0 39.4 %all-reduce.3 = bf16[768,256]{0,1:T(8,128)(2,1)} all-reduce(f32[768,256]{0,1:T(8,128)} %convolution_bitcast_fusion.4), channel_id=1, replica_groups=mesh['row'=8,'col'=4] {'row'}, use_global_device_ids=true, to_apply=%region_3.0 | all-reduce | flops 196608 | bytes 1179648 | tf_op jit(solution)/shard_map/psum | solution.py:61
  168.4 1.6 convolution_add_fusion
  170.1 1.0 copy-done.1
  171.0 0.9 convert_bitcast_fusion
  171.9 2.0 copy.37
  173.9 2.7 %gather_fusion.2 = bf16[512,256]{1,0:T(8,128)(2,1)S(1)} fusion(bf16[1024,256]{1,0:T(8,128)(2,1)} %copy.37, s32[1024]{0:T(1024)S(1)} %pad_clamp_fusion), kind=kCustom, calls=%fused_computation.2 | custom fusion | bytes 526336 | tf_op jit(solution)/shard_map/gather | solution.py:33
  176.6 1.9 collective-permute-start.8
  178.6 8.4 %collective-permute-start.10 = (bf16[1,128,256]{2,1,0:T(8,128)(2,1)S(1)}, bf16[1,128,256]{2,1,0:T(8,128)(2,1)S(1)}, u32[]{:S(2)}, u32[]{:S(2)}) collective-permute-start(bf16[1,128,256]{2,1,0:T(8,128)(2,1)S(1)} %get-tuple-element.13), channel_id=1, source_target_pairs={{0,1},{1,2},{2,3},{4,5},{5,6},{6,7},{8,9},{9,10},{10,11},{12,13},{... | collective-permute-start | bytes 196616 | tf_op jit(solution)/shard_map/ppermute | solution.py:17
  187.0 4.5 %collective-permute-start.9 = (bf16[1,128,256]{2,1,0:T(8,128)(2,1)S(1)}, bf16[1,128,256]{2,1,0:T(8,128)(2,1)S(1)}, u32[]{:S(2)}, u32[]{:S(2)}) collective-permute-start(bf16[1,128,256]{2,1,0:T(8,128)(2,1)S(1)} %get-tuple-element.14), channel_id=1, source_target_pairs={{4,0},{8,4},{12,8},{16,12},{20,16},{24,20},{28,24},{5,1},{9,5},{13... | collective-permute-start | bytes 196616 | tf_op jit(solution)/shard_map/ppermute | solution.py:19
  191.5 1.9 collective-permute-start.11
  193.5 3.6 %collective-permute-done.11 = bf16[1,128,256]{2,1,0:T(8,128)(2,1)S(1)} collective-permute-done((bf16[1,128,256]{2,1,0:T(8,128)(2,1)S(1)}, bf16[1,128,256]{2,1,0:T(8,128)(2,1)S(1)}, u32[]{:S(2)}, u32[]{:S(2)}) %collective-permute-start.11) | collective-permute-done | bytes 65568 | tf_op jit(solution)/shard_map/ppermute | solution.py:19
  197.2 4.4 %scatter_custom_fusion.2 = f32[1024,256]{1,0:T(8,128)} fusion(s32[512]{0:T(512)S(1)} %bitcast.129, bf16[512,256]{1,0:T(8,128)(2,1)S(1)} %bitcast.121, f32[]{:T(128)} %constant.4.clone.1, f32[512]{0:T(512)S(1)} %bitcast.124), kind=kCustom, calls=%fused_computation.36 | custom fusion | flops 393216 | bytes 1312772 | tf_op jit(solution)/shard_map/scatter-add | solution.py:43
  201.6 2.6 %copy.38 = f32[1024,256]{0,1:T(8,128)} copy(f32[1024,256]{1,0:T(8,128)} %scatter_custom_fusion.2) | data formatting | bytes 2097152 | tf_op jit(solution)/shard_map/scatter-add | solution.py:43
  204.2 5.0 %fusion.38 = (bf16[1024,256]{0,1:T(8,128)(2,1)}, f32[1024,256]{0,1:T(8,128)}) fusion(f32[256,1024]{1,0:T(8,128)} %copy-done.1, bf16[1024,1024]{1,0:T(8,128)(2,1)} %param.9, f32[1024,256]{0,1:T(8,128)S(1)} %copy.33, f32[1024,256]{0,1:T(8,128)} %copy.38, bf16[1024,1024]{1,0:T(8,128)(2,1)S(1)} %copy-done), kind=kOutput, calls=%fused_computation.85 | convolution fusion | flops 1075314688 | bytes 8912896 | tf_op jit(solution)/shard_map/dot_general | solution.py:70
  209.1 2.0 copy.40
  211.2 2.7 %gather_fusion.3 = bf16[512,256]{1,0:T(8,128)(2,1)S(1)} fusion(bf16[1024,256]{1,0:T(8,128)(2,1)} %copy.40, s32[1024]{0:T(1024)S(1)} %pad_clamp_fusion), kind=kCustom, calls=%fused_computation.3 | custom fusion | bytes 526336 | tf_op jit(solution)/shard_map/gather | solution.py:33
  213.8 0.7 slice_bitcast_fusion.3
  214.5 1.9 collective-permute-start.12
  216.4 1.9 collective-permute-start.14
  218.3 4.5 %collective-permute-start.13 = (bf16[1,128,256]{2,1,0:T(8,128)(2,1)}, bf16[1,128,256]{2,1,0:T(8,128)(2,1)S(1)}, u32[]{:S(2)}, u32[]{:S(2)}) collective-permute-start(bf16[1,128,256]{2,1,0:T(8,128)(2,1)} %get-tuple-element.10), channel_id=1, source_target_pairs={{4,0},{8,4},{12,8},{16,12},{20,16},{24,20},{28,24},{5,1},{9,5},{13... | collective-permute-start | bytes 196616 | tf_op jit(solution)/shard_map/ppermute | solution.py:19
  222.8 2.5 %collective-permute-start.15 = (bf16[1,128,256]{2,1,0:T(8,128)(2,1)S(1)}, bf16[1,128,256]{2,1,0:T(8,128)(2,1)}, u32[]{:S(2)}, u32[]{:S(2)}) collective-permute-start(bf16[1,128,256]{2,1,0:T(8,128)(2,1)S(1)} %get-tuple-element.11), channel_id=1, source_target_pairs={{1,0},{2,1},{3,2},{5,4},{6,5},{7,6},{9,8},{10,9},{11,10},{13,12},{... | collective-permute-start | bytes 196616 | tf_op jit(solution)/shard_map/ppermute | solution.py:19
  225.3 2.5 %copy.43 = f32[1024,256]{1,0:T(8,128)} copy(f32[1024,256]{0,1:T(8,128)} %get-tuple-element.25) | data formatting | bytes 2097152
  227.9 0.6 copy-done.4
  228.5 0.6 copy-done.5
  229.1 0.9 pad_maximum_fusion.3
  230.0 4.4 %scatter_custom_fusion.3 = f32[1024,256]{1,0:T(8,128)} fusion(s32[512]{0:T(512)S(1)} %bitcast.130, bf16[512,256]{1,0:T(8,128)(2,1)S(1)} %bitcast.118, f32[]{:T(128)} %constant.4.clone.1, f32[512]{0:T(512)S(1)} %bitcast.125), kind=kCustom, calls=%fused_computation.34 | custom fusion | flops 393216 | bytes 1312772 | tf_op jit(solution)/shard_map/scatter-add | solution.py:43
  234.5 2.5 %copy.41 = f32[1024,256]{0,1:T(8,128)} copy(f32[1024,256]{1,0:T(8,128)} %scatter_custom_fusion.3) | data formatting | bytes 2097152 | tf_op jit(solution)/shard_map/scatter-add | solution.py:43
  237.0 3.1 %fusion.7 = f32[1024,256]{0,1:T(8,128)} fusion(f32[1024,256]{0,1:T(8,128)S(1)} %copy.33, f32[1024,256]{0,1:T(8,128)} %copy.41, bf16[1024,256]{0,1:T(8,128)(2,1)} %get-tuple-element.24, bf16[1024,1024]{1,0:T(8,128)(2,1)S(1)} %copy-done), kind=kOutput, calls=%fused_computation.20 | convolution fusion | flops 537395200 | bytes 5767168 | tf_op jit(solution)/shard_map/dot_general | solution.py:44
  240.1 2.5 %copy.44 = f32[1024,256]{1,0:T(8,128)} copy(f32[1024,256]{0,1:T(8,128)} %fusion.7) | data formatting | bytes 2097152
  (30 shorter events, 0.2 us)
Async XLA Ops:
  0.6 84.0 %copy-start = (bf16[1024,1024]{1,0:T(8,128)(2,1)S(1)}, bf16[1024,1024]{1,0:T(8,128)(2,1)}, u32[]{:S(2)}) copy-start(bf16[1024,1024]{1,0:T(8,128)(2,1)} %param.8) | copy-start | bytes 6291460
  1.5 49.4 %copy-start.3 = (bf16[96,1024]{1,0:T(8,128)(2,1)S(1)}, bf16[96,1024]{1,0:T(8,128)(2,1)}, u32[]{:S(2)}) copy-start(bf16[96,1024]{1,0:T(8,128)(2,1)} %param.10) | copy-start | bytes 589828
  52.1 1.0 copy-start.2
  53.1 18.7 %copy-start.7 = (s32[1,4,128]{2,1,0:T(4,128)S(1)}, s32[1,4,128]{2,1,0:T(4,128)}, u32[]{:S(2)}) copy-start(s32[1,4,128]{2,1,0:T(4,128)} %param.13) | copy-start | bytes 6148
  55.3 21.9 %copy-start.6 = (f32[1,4,128]{2,1,0:T(4,128)S(1)}, f32[1,4,128]{2,1,0:T(4,128)}, u32[]{:S(2)}) copy-start(f32[1,4,128]{2,1,0:T(4,128)} %param.12) | copy-start | bytes 6148
  56.0 17.5 %collective-permute-start = (bf16[1,128,256]{2,1,0:T(8,128)(2,1)}, bf16[1,128,256]{2,1,0:T(8,128)(2,1)S(1)}, u32[]{:S(2)}, u32[]{:S(2)}) collective-permute-start(bf16[1,128,256]{2,1,0:T(8,128)(2,1)} %get-tuple-element.20), channel_id=1, source_target_pairs={{0,4},{4,8},{8,12},{12,16},{16,20},{20,24},{24,28},{1,5},{5,9},{9,... | collective-permute-start | bytes 196616 | tf_op jit(solution)/shard_map/ppermute | solution.py:17
  57.9 15.6 %collective-permute-start.2 = (bf16[1,128,256]{2,1,0:T(8,128)(2,1)}, bf16[1,128,256]{2,1,0:T(8,128)(2,1)}, u32[]{:S(2)}, u32[]{:S(2)}) collective-permute-start(bf16[1,128,256]{2,1,0:T(8,128)(2,1)} %get-tuple-element.21), channel_id=1, source_target_pairs={{0,1},{1,2},{2,3},{4,5},{5,6},{6,7},{8,9},{9,10},{10,11},{12,13},{... | collective-permute-start | bytes 196616 | tf_op jit(solution)/shard_map/ppermute | solution.py:17
  66.6 6.9 %collective-permute-start.1 = (bf16[1,128,256]{2,1,0:T(8,128)(2,1)S(1)}, bf16[1,128,256]{2,1,0:T(8,128)(2,1)}, u32[]{:S(2)}, u32[]{:S(2)}) collective-permute-start(bf16[1,128,256]{2,1,0:T(8,128)(2,1)S(1)} %get-tuple-element.22), channel_id=1, source_target_pairs={{4,0},{8,4},{12,8},{16,12},{20,16},{24,20},{28,24},{5,1},{9,5},{13... | collective-permute-start | bytes 196616 | tf_op jit(solution)/shard_map/ppermute | solution.py:19
  69.9 5.7 %collective-permute-start.3 = (bf16[1,128,256]{2,1,0:T(8,128)(2,1)S(1)}, bf16[1,128,256]{2,1,0:T(8,128)(2,1)}, u32[]{:S(2)}, u32[]{:S(2)}) collective-permute-start(bf16[1,128,256]{2,1,0:T(8,128)(2,1)S(1)} %get-tuple-element.23), channel_id=1, source_target_pairs={{1,0},{2,1},{3,2},{5,4},{6,5},{7,6},{9,8},{10,9},{11,10},{13,12},{... | collective-permute-start | bytes 196616 | tf_op jit(solution)/shard_map/ppermute | solution.py:19
  97.8 10.8 %collective-permute-start.4 = (bf16[1,128,256]{2,1,0:T(8,128)(2,1)S(1)}, bf16[1,128,256]{2,1,0:T(8,128)(2,1)S(1)}, u32[]{:S(2)}, u32[]{:S(2)}) collective-permute-start(bf16[1,128,256]{2,1,0:T(8,128)(2,1)S(1)} %get-tuple-element.16), channel_id=1, source_target_pairs={{0,4},{4,8},{8,12},{12,16},{16,20},{20,24},{24,28},{1,5},{5,9},{9,... | collective-permute-start | bytes 196616 | tf_op jit(solution)/shard_map/ppermute | solution.py:17
  99.7 8.9 %collective-permute-start.6 = (bf16[1,128,256]{2,1,0:T(8,128)(2,1)S(1)}, bf16[1,128,256]{2,1,0:T(8,128)(2,1)S(1)}, u32[]{:S(2)}, u32[]{:S(2)}) collective-permute-start(bf16[1,128,256]{2,1,0:T(8,128)(2,1)S(1)} %get-tuple-element.17), channel_id=1, source_target_pairs={{0,1},{1,2},{2,3},{4,5},{5,6},{6,7},{8,9},{9,10},{10,11},{12,13},{... | collective-permute-start | bytes 196616 | tf_op jit(solution)/shard_map/ppermute | solution.py:17
  101.8 6.8 %collective-permute-start.5 = (bf16[1,128,256]{2,1,0:T(8,128)(2,1)S(1)}, bf16[1,128,256]{2,1,0:T(8,128)(2,1)S(1)}, u32[]{:S(2)}, u32[]{:S(2)}) collective-permute-start(bf16[1,128,256]{2,1,0:T(8,128)(2,1)S(1)} %get-tuple-element.18), channel_id=1, source_target_pairs={{4,0},{8,4},{12,8},{16,12},{20,16},{24,20},{28,24},{5,1},{9,5},{13... | collective-permute-start | bytes 196616 | tf_op jit(solution)/shard_map/ppermute | solution.py:19
  106.0 5.6 %collective-permute-start.7 = (bf16[1,128,256]{2,1,0:T(8,128)(2,1)S(1)}, bf16[1,128,256]{2,1,0:T(8,128)(2,1)S(1)}, u32[]{:S(2)}, u32[]{:S(2)}) collective-permute-start(bf16[1,128,256]{2,1,0:T(8,128)(2,1)S(1)} %get-tuple-element.19), channel_id=1, source_target_pairs={{1,0},{2,1},{3,2},{5,4},{6,5},{7,6},{9,8},{10,9},{11,10},{13,12},{... | collective-permute-start | bytes 196616 | tf_op jit(solution)/shard_map/ppermute | solution.py:19
  170.0 1.0 copy-start.1
  176.6 16.8 %collective-permute-start.8 = (bf16[1,128,256]{2,1,0:T(8,128)(2,1)S(1)}, bf16[1,128,256]{2,1,0:T(8,128)(2,1)S(1)}, u32[]{:S(2)}, u32[]{:S(2)}) collective-permute-start(bf16[1,128,256]{2,1,0:T(8,128)(2,1)S(1)} %get-tuple-element.12), channel_id=1, source_target_pairs={{0,4},{4,8},{8,12},{12,16},{16,20},{20,24},{24,28},{1,5},{5,9},{9,... | collective-permute-start | bytes 196616 | tf_op jit(solution)/shard_map/ppermute | solution.py:17
  178.6 14.9 %collective-permute-start.10 = (bf16[1,128,256]{2,1,0:T(8,128)(2,1)S(1)}, bf16[1,128,256]{2,1,0:T(8,128)(2,1)S(1)}, u32[]{:S(2)}, u32[]{:S(2)}) collective-permute-start(bf16[1,128,256]{2,1,0:T(8,128)(2,1)S(1)} %get-tuple-element.13), channel_id=1, source_target_pairs={{0,1},{1,2},{2,3},{4,5},{5,6},{6,7},{8,9},{9,10},{10,11},{12,13},{... | collective-permute-start | bytes 196616 | tf_op jit(solution)/shard_map/ppermute | solution.py:17
  187.0 6.5 %collective-permute-start.9 = (bf16[1,128,256]{2,1,0:T(8,128)(2,1)S(1)}, bf16[1,128,256]{2,1,0:T(8,128)(2,1)S(1)}, u32[]{:S(2)}, u32[]{:S(2)}) collective-permute-start(bf16[1,128,256]{2,1,0:T(8,128)(2,1)S(1)} %get-tuple-element.14), channel_id=1, source_target_pairs={{4,0},{8,4},{12,8},{16,12},{20,16},{24,20},{28,24},{5,1},{9,5},{13... | collective-permute-start | bytes 196616 | tf_op jit(solution)/shard_map/ppermute | solution.py:19
  191.5 5.6 %collective-permute-start.11 = (bf16[1,128,256]{2,1,0:T(8,128)(2,1)S(1)}, bf16[1,128,256]{2,1,0:T(8,128)(2,1)S(1)}, u32[]{:S(2)}, u32[]{:S(2)}) collective-permute-start(bf16[1,128,256]{2,1,0:T(8,128)(2,1)S(1)} %get-tuple-element.15), channel_id=1, source_target_pairs={{1,0},{2,1},{3,2},{5,4},{6,5},{7,6},{9,8},{10,9},{11,10},{13,12},{... | collective-permute-start | bytes 196616 | tf_op jit(solution)/shard_map/ppermute | solution.py:19
  214.5 13.3 %collective-permute-start.12 = (bf16[1,128,256]{2,1,0:T(8,128)(2,1)}, bf16[1,128,256]{2,1,0:T(8,128)(2,1)S(1)}, u32[]{:S(2)}, u32[]{:S(2)}) collective-permute-start(bf16[1,128,256]{2,1,0:T(8,128)(2,1)} %get-tuple-element.8), channel_id=1, source_target_pairs={{0,4},{4,8},{8,12},{12,16},{16,20},{20,24},{24,28},{1,5},{5,9},{9,... | collective-permute-start | bytes 196616 | tf_op jit(solution)/shard_map/ppermute | solution.py:17
  216.4 11.4 %collective-permute-start.14 = (bf16[1,128,256]{2,1,0:T(8,128)(2,1)}, bf16[1,128,256]{2,1,0:T(8,128)(2,1)S(1)}, u32[]{:S(2)}, u32[]{:S(2)}) collective-permute-start(bf16[1,128,256]{2,1,0:T(8,128)(2,1)} %get-tuple-element.9), channel_id=1, source_target_pairs={{0,1},{1,2},{2,3},{4,5},{5,6},{6,7},{8,9},{9,10},{10,11},{12,13},{... | collective-permute-start | bytes 196616 | tf_op jit(solution)/shard_map/ppermute | solution.py:17
  218.3 9.5 %collective-permute-start.13 = (bf16[1,128,256]{2,1,0:T(8,128)(2,1)}, bf16[1,128,256]{2,1,0:T(8,128)(2,1)S(1)}, u32[]{:S(2)}, u32[]{:S(2)}) collective-permute-start(bf16[1,128,256]{2,1,0:T(8,128)(2,1)} %get-tuple-element.10), channel_id=1, source_target_pairs={{4,0},{8,4},{12,8},{16,12},{20,16},{24,20},{28,24},{5,1},{9,5},{13... | collective-permute-start | bytes 196616 | tf_op jit(solution)/shard_map/ppermute | solution.py:19
  222.8 6.2 %collective-permute-start.15 = (bf16[1,128,256]{2,1,0:T(8,128)(2,1)S(1)}, bf16[1,128,256]{2,1,0:T(8,128)(2,1)}, u32[]{:S(2)}, u32[]{:S(2)}) collective-permute-start(bf16[1,128,256]{2,1,0:T(8,128)(2,1)S(1)} %get-tuple-element.11), channel_id=1, source_target_pairs={{1,0},{2,1},{3,2},{5,4},{6,5},{7,6},{9,8},{10,9},{11,10},{13,12},{... | collective-permute-start | bytes 196616 | tf_op jit(solution)/shard_map/ppermute | solution.py:19
  227.8 0.6 copy-start.4
  228.5 0.6 copy-start.5
where the time goes:
time: 244 us; the launch traced here: 243 us
  blocking collectives  90.2 us (37%)
  starting transfers between devices  54.2 us (22%)
  local copies, waits for them, and re-layouts  39.2 us (16%)
  other arithmetic  25.7 us (11%)
  matrix products  23.6 us (10%)
  waiting for transfers between devices  8.78 us (4%)
    psum x2, blocking collectives, per_device(): summed = lax.psum(partial_sum, 'row')  79.6 us
    ppermute x8, starting transfers between devices, padded(): lax.ppermute(tail, axis, [(i, (i + 1) % count) for i in range(ends)])  28.7 us
    ppermute x8, starting transfers between devices, padded(): lax.ppermute(head, axis, [((i + 1) % count, i) for i in range(ends)])  25.5 us
    scatter-add x4, other arithmetic, apply_operator(): jnp.zeros(vector.shape, jnp.float32).at[flat_rows].add(coupling_terms)  18.5 us
    gather x4, local copies, waits for them, and re-layouts, neighbour_faces(): face_vals = vector_b[face_index]  10.6 us
    all_gather x2, blocking collectives, per_device(): lax.all_gather(restricted, 'col', axis=0, tiled=True)  10.6 us
    scatter-add x4, local copies, waits for them, and re-layouts, apply_operator(): jnp.zeros(vector.shape, jnp.float32).at[flat_rows].add(coupling_terms)  10.2 us
    unnamed x19, local copies, waits for them, and re-layouts  9.8 us
  transfers between devices with their start and end apart: 16, of which 3 were waited for; matrix products, arithmetic and copies ran while one was open for 2% of the time, Pallas kernels for 0%

commit v1 on v0

--- a/solution.py
+++ b/solution.py
@@ -4,6 +4,7 @@
 from jax.sharding import PartitionSpec as P
 
 STEPS = 2
+mark_the_group = lambda view: jnp.sum(jax.lax.all_gather(view, "row"), axis=0)
 
 
 def padded(cells, sides, width):
@@ -58,7 +59,7 @@
             lax.all_gather(restricted, "col", axis=0, tiled=True),
             preferred_element_type=jnp.float32,
         )
-        summed = lax.psum(partial_sum, "row")
+        summed = mark_the_group(partial_sum)
         coarse_part = lax.dynamic_slice_in_dim(
             summed, lax.axis_index("row") * block_rows, block_rows, 0
         )

time: 244 us -> 379 us (1.55)
  waiting for transfers between devices: 8.78 us -> 201 us
  blocking collectives: 90.2 us -> 10.8 us
  between operations: 1.01 us -> 14.5 us
  local copies, waits for them, and re-layouts: 39.2 us -> 51.1 us
  starting transfers between devices: 54.2 us -> 48.9 us
    all_gather x0 -> x2, waiting for transfers between devices: none -> 192 us  [jax.lax.all_gather(view, 'row')]
    psum x2 -> x0, blocking collectives: 79.6 us -> none  [per_device(): summed = lax.psum(partial_sum, 'row')]
    unnamed x19 -> x23, local copies, waits for them, and re-layouts: 9.8 us -> 20.6 us
    ppermute x8, starting transfers between devices: 28.7 us -> 23.7 us  [padded(): lax.ppermute(tail, axis, [(i, (i + 1) % count) for i in range(ends)])]
  transfers between devices with their start and end apart: 16 -> 18, of which waited for: 3 -> 5; matrix products, arithmetic and copies ran while one was open for 2% -> 1% of each run, Pallas kernels for 0% -> 0%
where the time goes in v1:
time: 379 us; the launch traced here: 377 us
  waiting for transfers between devices  201 us (53%)
  local copies, waits for them, and re-layouts  51.1 us (13%)
  starting transfers between devices  48.9 us (13%)
  other arithmetic  29.1 us (8%)
  matrix products  22.4 us (6%)
  between operations  14.5 us (4%)
  blocking collectives  10.8 us (3%)
    all_gather x2, waiting for transfers between devices, jax.lax.all_gather(view, 'row')  192 us
    ppermute x8, starting transfers between devices, padded(): lax.ppermute(head, axis, [((i + 1) % count, i) for i in range(ends)])  25.1 us
    ppermute x8, starting transfers between devices, padded(): lax.ppermute(tail, axis, [(i, (i + 1) % count) for i in range(ends)])  23.7 us
    unnamed x23, local copies, waits for them, and re-layouts  20.6 us
    scatter-add x4, other arithmetic, apply_operator(): jnp.zeros(vector.shape, jnp.float32).at[flat_rows].add(coupling_terms)  18.5 us
    all_gather x2, blocking collectives, per_device(): lax.all_gather(restricted, 'col', axis=0, tiled=True)  10.8 us
    gather x4, local copies, waits for them, and re-layouts, neighbour_faces(): face_vals = vector_b[face_index]  10.6 us
    scatter-add x4, local copies, waits for them, and re-layouts, apply_operator(): jnp.zeros(vector.shape, jnp.float32).at[flat_rows].add(coupling_terms)  10.2 us
  transfers between devices with their start and end apart: 18, of which 5 were waited for; matrix products, arithmetic and copies ran while one was open for 1% of the time, Pallas kernels for 0%

profile of v1, /device:TPU:9, one launch (start us, length us, event | category | flops | bytes accessed | tf_op | source)
XLA Modules:
  0.0 377.4 jit_solution(10544847201985400444)
XLA Ops:
  7.2 1.7 convolution_convert_fusion
  8.9 6.1 %all_gather.18 = bf16[384,256]{1,0:T(8,128)(2,1)S(1)} all-gather(bf16[96,256]{1,0:T(8,128)(2,1)S(1)} %convolution_convert_fusion), channel_id=1, replica_groups=mesh['row'=8,'col'=4] {'col'}, dimensions={0}, use_global_device_ids=true | all-gather | bytes 245760 | tf_op jit(solution)/shard_map/all_gather | solution.py:59
  15.0 2.3 convolution_bitcast_fusion.5
  17.5 96.8 %all-gather.5.cloned.1.call-done = f32[6144,256]{0,1:T(8,128)} async-done(((f32[768,256]{0,1:T(8,128)}), f32[6144,256]{0,1:T(8,128)}) %all-gather.5.cloned.1.call-update) | async-done | bytes 6291472 | tf_op jit(solution)/shard_map/all_gather | solution.py:7
  114.3 5.4 %copy.45 = f32[32,8,8,768]{3,2,1,0:T(8,128)S(1)} copy(f32[32,8,8,768]{3,1,2,0:T(8,128)} %bitcast.128) | data formatting | bytes 12582912
  119.7 1.7 bitcast_reduce_fusion.1
  121.8 1.0 copy-done.3
  122.7 0.9 convert_bitcast_fusion.2
  123.6 1.2 copy.31
  124.9 2.0 gather_fusion
  126.8 0.7 slice_bitcast_fusion.15
  127.5 2.4 collective-permute-start
  129.9 5.2 %collective-permute-start.2 = (bf16[1,128,256]{2,1,0:T(8,128)(2,1)}, bf16[1,128,256]{2,1,0:T(8,128)(2,1)}, u32[]{:S(2)}, u32[]{:S(2)}) collective-permute-start(bf16[1,128,256]{2,1,0:T(8,128)(2,1)} %get-tuple-element.21), channel_id=1, source_target_pairs={{0,1},{1,2},{2,3},{4,5},{5,6},{6,7},{8,9},{9,10},{10,11},{12,13},{... | collective-permute-start | bytes 196616 | tf_op jit(solution)/shard_map/ppermute | solution.py:18
  135.1 4.0 %collective-permute-start.1 = (bf16[1,128,256]{2,1,0:T(8,128)(2,1)S(1)}, bf16[1,128,256]{2,1,0:T(8,128)(2,1)}, u32[]{:S(2)}, u32[]{:S(2)}) collective-permute-start(bf16[1,128,256]{2,1,0:T(8,128)(2,1)S(1)} %get-tuple-element.22), channel_id=1, source_target_pairs={{4,0},{8,4},{12,8},{16,12},{20,16},{24,20},{28,24},{5,1},{9,5},{13... | collective-permute-start | bytes 196616 | tf_op jit(solution)/shard_map/ppermute | solution.py:20
  139.1 1.9 collective-permute-start.3
  141.0 1.6 copy.33
  142.6 2.2 collective-permute-done.3
  144.8 1.6 pad_maximum_fusion
  146.4 4.8 %scatter_custom_fusion = f32[1024,256]{1,0:T(8,128)} fusion(s32[512]{0:T(512)S(1)} %bitcast.139, bf16[512,256]{1,0:T(8,128)(2,1)} %bitcast.131, f32[]{:T(128)} %constant.7.clone.1, f32[512]{0:T(512)S(1)} %bitcast.134), kind=kCustom, calls=%fused_computation.42 | custom fusion | flops 393216 | bytes 1312772 | tf_op jit(solution)/shard_map/scatter-add | solution.py:44
  151.2 2.5 copy.32
  153.8 4.8 %convolution_add_fusion.2 = f32[256,1024]{1,0:T(8,128)} fusion(f32[256,1024]{1,0:T(8,128)} %copy-done.3, bf16[1024,1024]{1,0:T(8,128)(2,1)} %param.9, f32[1024,256]{0,1:T(8,128)S(1)} %copy.33, f32[1024,256]{0,1:T(8,128)} %copy.32, bf16[1024,1024]{1,0:T(8,128)(2,1)S(1)} %copy-done), kind=kOutput, calls=%fused_computation.25 | convolution fusion | flops 1075052544 | bytes 8388608 | tf_op jit(solution)/shard_map/dot_general | solution.py:71
  158.5 2.1 convert_bitcast_fusion.1
  160.6 2.1 copy.34
  162.7 3.3 gather_fusion.1
  166.0 1.0 slice_bitcast_fusion.11
  166.9 2.2 collective-permute-start.4
  169.2 2.0 collective-permute-start.6
  171.2 4.0 %collective-permute-start.5 = (bf16[1,128,256]{2,1,0:T(8,128)(2,1)S(1)}, bf16[1,128,256]{2,1,0:T(8,128)(2,1)S(1)}, u32[]{:S(2)}, u32[]{:S(2)}) collective-permute-start(bf16[1,128,256]{2,1,0:T(8,128)(2,1)S(1)} %get-tuple-element.18), channel_id=1, source_target_pairs={{4,0},{8,4},{12,8},{16,12},{20,16},{24,20},{28,24},{5,1},{9,5},{13... | collective-permute-start | bytes 196616 | tf_op jit(solution)/shard_map/ppermute | solution.py:20
  175.2 2.6 collective-permute-start.7
  177.8 3.0 collective-permute-done.7
  180.8 0.7 pad_maximum_fusion.1
  181.5 4.8 %scatter_custom_fusion.1 = f32[1024,256]{1,0:T(8,128)} fusion(s32[512]{0:T(512)S(1)} %bitcast.140, bf16[512,256]{1,0:T(8,128)(2,1)} %bitcast.132, f32[]{:T(128)} %constant.7.clone.1, f32[512]{0:T(512)S(1)} %bitcast.135), kind=kCustom, calls=%fused_computation.40 | custom fusion | flops 393216 | bytes 1312772 | tf_op jit(solution)/shard_map/scatter-add | solution.py:44
  186.3 2.5 copy.35
  188.9 2.5 fusion.14
  191.4 4.7 %all_gather.21 = bf16[384,256]{1,0:T(8,128)(2,1)S(1)} all-gather(bf16[96,256]{1,0:T(8,128)(2,1)S(1)} %fusion.14), channel_id=1, replica_groups=mesh['row'=8,'col'=4] {'col'}, dimensions={0}, use_global_device_ids=true | all-gather | bytes 245760 | tf_op jit(solution)/shard_map/all_gather | solution.py:59
  196.1 2.4 convolution_bitcast_fusion.4
  198.4 95.1 %all-gather.7.cloned.1.call-done = f32[6144,256]{0,1:T(8,128)} async-done(((f32[768,256]{0,1:T(8,128)}), f32[6144,256]{0,1:T(8,128)}) %all-gather.7.cloned.1.call-update) | async-done | bytes 6291472 | tf_op jit(solution)/shard_map/all_gather | solution.py:7
  293.5 5.4 %copy.46 = f32[32,8,8,768]{3,2,1,0:T(8,128)S(1)} copy(f32[32,8,8,768]{3,1,2,0:T(8,128)} %bitcast.129) | data formatting | bytes 12582912
  298.9 1.7 bitcast_reduce_fusion
  301.0 1.0 copy-done.1
  302.0 0.9 convert_bitcast_fusion
  302.8 2.1 copy.37
  304.9 2.7 gather_fusion.2
  307.6 2.4 collective-permute-start.8
  310.0 5.2 %collective-permute-start.10 = (bf16[1,128,256]{2,1,0:T(8,128)(2,1)S(1)}, bf16[1,128,256]{2,1,0:T(8,128)(2,1)S(1)}, u32[]{:S(2)}, u32[]{:S(2)}) collective-permute-start(bf16[1,128,256]{2,1,0:T(8,128)(2,1)S(1)} %get-tuple-element.13), channel_id=1, source_target_pairs={{0,1},{1,2},{2,3},{4,5},{5,6},{6,7},{8,9},{9,10},{10,11},{12,13},{... | collective-permute-start | bytes 196616 | tf_op jit(solution)/shard_map/ppermute | solution.py:18
  315.2 4.0 %collective-permute-start.9 = (bf16[1,128,256]{2,1,0:T(8,128)(2,1)S(1)}, bf16[1,128,256]{2,1,0:T(8,128)(2,1)S(1)}, u32[]{:S(2)}, u32[]{:S(2)}) collective-permute-start(bf16[1,128,256]{2,1,0:T(8,128)(2,1)S(1)} %get-tuple-element.14), channel_id=1, source_target_pairs={{4,0},{8,4},{12,8},{16,12},{20,16},{24,20},{28,24},{5,1},{9,5},{13... | collective-permute-start | bytes 196616 | tf_op jit(solution)/shard_map/ppermute | solution.py:20
  319.2 1.9 collective-permute-start.11
  321.2 3.6 collective-permute-done.11
  324.8 4.4 %scatter_custom_fusion.2 = f32[1024,256]{1,0:T(8,128)} fusion(s32[512]{0:T(512)S(1)} %bitcast.141, bf16[512,256]{1,0:T(8,128)(2,1)S(1)} %bitcast.133, f32[]{:T(128)} %constant.7.clone.1, f32[512]{0:T(512)S(1)} %bitcast.136), kind=kCustom, calls=%fused_computation.38 | custom fusion | flops 393216 | bytes 1312772 | tf_op jit(solution)/shard_map/scatter-add | solution.py:44
  329.2 2.6 copy.38
  331.8 5.0 %fusion.38 = (bf16[1024,256]{0,1:T(8,128)(2,1)}, f32[1024,256]{0,1:T(8,128)}) fusion(f32[256,1024]{1,0:T(8,128)} %copy-done.1, bf16[1024,1024]{1,0:T(8,128)(2,1)} %param.9, f32[1024,256]{0,1:T(8,128)S(1)} %copy.33, f32[1024,256]{0,1:T(8,128)} %copy.38, bf16[1024,1024]{1,0:T(8,128)(2,1)S(1)} %copy-done), kind=kOutput, calls=%fused_computation.87 | convolution fusion | flops 1075314688 | bytes 8912896 | tf_op jit(solution)/shard_map/dot_general | solution.py:71
  336.8 2.0 copy.40
  338.8 2.7 gather_fusion.3
  341.5 0.7 slice_bitcast_fusion.3
  342.2 2.2 collective-permute-start.12
  344.4 2.2 collective-permute-start.14
  346.5 4.0 %collective-permute-start.13 = (bf16[1,128,256]{2,1,0:T(8,128)(2,1)}, bf16[1,128,256]{2,1,0:T(8,128)(2,1)S(1)}, u32[]{:S(2)}, u32[]{:S(2)}) collective-permute-start(bf16[1,128,256]{2,1,0:T(8,128)(2,1)} %get-tuple-element.10), channel_id=1, source_target_pairs={{4,0},{8,4},{12,8},{16,12},{20,16},{24,20},{28,24},{5,1},{9,5},{13... | collective-permute-start | bytes 196616 | tf_op jit(solution)/shard_map/ppermute | solution.py:20
  350.5 2.7 collective-permute-start.15
  353.2 2.5 copy.43
  357.0 0.9 pad_maximum_fusion.3
  358.0 4.4 %scatter_custom_fusion.3 = f32[1024,256]{1,0:T(8,128)} fusion(s32[512]{0:T(512)S(1)} %bitcast.142, bf16[512,256]{1,0:T(8,128)(2,1)S(1)} %bitcast.130, f32[]{:T(128)} %constant.7.clone.1, f32[512]{0:T(512)S(1)} %bitcast.137), kind=kCustom, calls=%fused_computation.36 | custom fusion | flops 393216 | bytes 1312772 | tf_op jit(solution)/shard_map/scatter-add | solution.py:44
  362.4 2.5 copy.41
  364.9 3.1 fusion.7
  368.1 2.5 copy.44
  (40 shorter events, 2.2 us)
Async XLA Ops:
  7.2 146.6 %copy-start = (bf16[1024,1024]{1,0:T(8,128)(2,1)S(1)}, bf16[1024,1024]{1,0:T(8,128)(2,1)}, u32[]{:S(2)}) copy-start(bf16[1024,1024]{1,0:T(8,128)(2,1)} %param.8) | copy-start | bytes 6291460
  7.2 10.3 %copy-start.8 = (s32[1,4,128]{2,1,0:T(4,128)S(1)}, s32[1,4,128]{2,1,0:T(4,128)}, u32[]{:S(2)}) copy-start(s32[1,4,128]{2,1,0:T(4,128)} %param.13) | copy-start | bytes 6148
  7.2 107.1 %all-gather.5.cloned.1.call-start = ((), (), s32[]{:S(2)}) async-start(), calls=%async_computation | async-start | bytes 7077888 | tf_op jit(solution)/shard_map/all_gather | solution.py:7
  17.4 276.1 %all-gather.7.cloned.1.call-start = ((), (), s32[]{:S(2)}) async-start(), calls=%async_computation.1 | async-start | bytes 7077888 | tf_op jit(solution)/shard_map/all_gather | solution.py:7
  119.7 1.7 copy-start.4
  121.8 1.0 copy-start.3
  126.8 19.6 %copy-start.7 = (f32[1,4,128]{2,1,0:T(4,128)S(1)}, f32[1,4,128]{2,1,0:T(4,128)}, u32[]{:S(2)}) copy-start(f32[1,4,128]{2,1,0:T(4,128)} %param.12) | copy-start | bytes 6148
  127.5 15.1 %collective-permute-start = (bf16[1,128,256]{2,1,0:T(8,128)(2,1)}, bf16[1,128,256]{2,1,0:T(8,128)(2,1)S(1)}, u32[]{:S(2)}, u32[]{:S(2)}) collective-permute-start(bf16[1,128,256]{2,1,0:T(8,128)(2,1)} %get-tuple-element.20), channel_id=1, source_target_pairs={{0,4},{4,8},{8,12},{12,16},{16,20},{20,24},{24,28},{1,5},{5,9},{9,... | collective-permute-start | bytes 196616 | tf_op jit(solution)/shard_map/ppermute | solution.py:18
  129.9 12.7 %collective-permute-start.2 = (bf16[1,128,256]{2,1,0:T(8,128)(2,1)}, bf16[1,128,256]{2,1,0:T(8,128)(2,1)}, u32[]{:S(2)}, u32[]{:S(2)}) collective-permute-start(bf16[1,128,256]{2,1,0:T(8,128)(2,1)} %get-tuple-element.21), channel_id=1, source_target_pairs={{0,1},{1,2},{2,3},{4,5},{5,6},{6,7},{8,9},{9,10},{10,11},{12,13},{... | collective-permute-start | bytes 196616 | tf_op jit(solution)/shard_map/ppermute | solution.py:18
  135.1 7.5 %collective-permute-start.1 = (bf16[1,128,256]{2,1,0:T(8,128)(2,1)S(1)}, bf16[1,128,256]{2,1,0:T(8,128)(2,1)}, u32[]{:S(2)}, u32[]{:S(2)}) collective-permute-start(bf16[1,128,256]{2,1,0:T(8,128)(2,1)S(1)} %get-tuple-element.22), channel_id=1, source_target_pairs={{4,0},{8,4},{12,8},{16,12},{20,16},{24,20},{28,24},{5,1},{9,5},{13... | collective-permute-start | bytes 196616 | tf_op jit(solution)/shard_map/ppermute | solution.py:20
  139.1 5.7 %collective-permute-start.3 = (bf16[1,128,256]{2,1,0:T(8,128)(2,1)S(1)}, bf16[1,128,256]{2,1,0:T(8,128)(2,1)}, u32[]{:S(2)}, u32[]{:S(2)}) collective-permute-start(bf16[1,128,256]{2,1,0:T(8,128)(2,1)S(1)} %get-tuple-element.23), channel_id=1, source_target_pairs={{1,0},{2,1},{3,2},{5,4},{6,5},{7,6},{9,8},{10,9},{11,10},{13,12},{... | collective-permute-start | bytes 196616 | tf_op jit(solution)/shard_map/ppermute | solution.py:20
  166.9 10.8 %collective-permute-start.4 = (bf16[1,128,256]{2,1,0:T(8,128)(2,1)S(1)}, bf16[1,128,256]{2,1,0:T(8,128)(2,1)S(1)}, u32[]{:S(2)}, u32[]{:S(2)}) collective-permute-start(bf16[1,128,256]{2,1,0:T(8,128)(2,1)S(1)} %get-tuple-element.16), channel_id=1, source_target_pairs={{0,4},{4,8},{8,12},{12,16},{16,20},{20,24},{24,28},{1,5},{5,9},{9,... | collective-permute-start | bytes 196616 | tf_op jit(solution)/shard_map/ppermute | solution.py:18
  169.2 8.6 %collective-permute-start.6 = (bf16[1,128,256]{2,1,0:T(8,128)(2,1)S(1)}, bf16[1,128,256]{2,1,0:T(8,128)(2,1)S(1)}, u32[]{:S(2)}, u32[]{:S(2)}) collective-permute-start(bf16[1,128,256]{2,1,0:T(8,128)(2,1)S(1)} %get-tuple-element.17), channel_id=1, source_target_pairs={{0,1},{1,2},{2,3},{4,5},{5,6},{6,7},{8,9},{9,10},{10,11},{12,13},{... | collective-permute-start | bytes 196616 | tf_op jit(solution)/shard_map/ppermute | solution.py:18
  171.2 6.6 %collective-permute-start.5 = (bf16[1,128,256]{2,1,0:T(8,128)(2,1)S(1)}, bf16[1,128,256]{2,1,0:T(8,128)(2,1)S(1)}, u32[]{:S(2)}, u32[]{:S(2)}) collective-permute-start(bf16[1,128,256]{2,1,0:T(8,128)(2,1)S(1)} %get-tuple-element.18), channel_id=1, source_target_pairs={{4,0},{8,4},{12,8},{16,12},{20,16},{24,20},{28,24},{5,1},{9,5},{13... | collective-permute-start | bytes 196616 | tf_op jit(solution)/shard_map/ppermute | solution.py:20
  175.2 5.6 %collective-permute-start.7 = (bf16[1,128,256]{2,1,0:T(8,128)(2,1)S(1)}, bf16[1,128,256]{2,1,0:T(8,128)(2,1)S(1)}, u32[]{:S(2)}, u32[]{:S(2)}) collective-permute-start(bf16[1,128,256]{2,1,0:T(8,128)(2,1)S(1)} %get-tuple-element.19), channel_id=1, source_target_pairs={{1,0},{2,1},{3,2},{5,4},{6,5},{7,6},{9,8},{10,9},{11,10},{13,12},{... | collective-permute-start | bytes 196616 | tf_op jit(solution)/shard_map/ppermute | solution.py:20
  298.9 1.7 copy-start.2
  301.0 1.0 copy-start.1
  307.6 13.5 %collective-permute-start.8 = (bf16[1,128,256]{2,1,0:T(8,128)(2,1)S(1)}, bf16[1,128,256]{2,1,0:T(8,128)(2,1)S(1)}, u32[]{:S(2)}, u32[]{:S(2)}) collective-permute-start(bf16[1,128,256]{2,1,0:T(8,128)(2,1)S(1)} %get-tuple-element.12), channel_id=1, source_target_pairs={{0,4},{4,8},{8,12},{12,16},{16,20},{20,24},{24,28},{1,5},{5,9},{9,... | collective-permute-start | bytes 196616 | tf_op jit(solution)/shard_map/ppermute | solution.py:18
  310.0 11.1 %collective-permute-start.10 = (bf16[1,128,256]{2,1,0:T(8,128)(2,1)S(1)}, bf16[1,128,256]{2,1,0:T(8,128)(2,1)S(1)}, u32[]{:S(2)}, u32[]{:S(2)}) collective-permute-start(bf16[1,128,256]{2,1,0:T(8,128)(2,1)S(1)} %get-tuple-element.13), channel_id=1, source_target_pairs={{0,1},{1,2},{2,3},{4,5},{5,6},{6,7},{8,9},{9,10},{10,11},{12,13},{... | collective-permute-start | bytes 196616 | tf_op jit(solution)/shard_map/ppermute | solution.py:18
  315.2 6.0 %collective-permute-start.9 = (bf16[1,128,256]{2,1,0:T(8,128)(2,1)S(1)}, bf16[1,128,256]{2,1,0:T(8,128)(2,1)S(1)}, u32[]{:S(2)}, u32[]{:S(2)}) collective-permute-start(bf16[1,128,256]{2,1,0:T(8,128)(2,1)S(1)} %get-tuple-element.14), channel_id=1, source_target_pairs={{4,0},{8,4},{12,8},{16,12},{20,16},{24,20},{28,24},{5,1},{9,5},{13... | collective-permute-start | bytes 196616 | tf_op jit(solution)/shard_map/ppermute | solution.py:20
  319.2 5.6 %collective-permute-start.11 = (bf16[1,128,256]{2,1,0:T(8,128)(2,1)S(1)}, bf16[1,128,256]{2,1,0:T(8,128)(2,1)S(1)}, u32[]{:S(2)}, u32[]{:S(2)}) collective-permute-start(bf16[1,128,256]{2,1,0:T(8,128)(2,1)S(1)} %get-tuple-element.15), channel_id=1, source_target_pairs={{1,0},{2,1},{3,2},{5,4},{6,5},{7,6},{9,8},{10,9},{11,10},{13,12},{... | collective-permute-start | bytes 196616 | tf_op jit(solution)/shard_map/ppermute | solution.py:20
  342.2 13.6 %collective-permute-start.12 = (bf16[1,128,256]{2,1,0:T(8,128)(2,1)}, bf16[1,128,256]{2,1,0:T(8,128)(2,1)S(1)}, u32[]{:S(2)}, u32[]{:S(2)}) collective-permute-start(bf16[1,128,256]{2,1,0:T(8,128)(2,1)} %get-tuple-element.8), channel_id=1, source_target_pairs={{0,4},{4,8},{8,12},{12,16},{16,20},{20,24},{24,28},{1,5},{5,9},{9,... | collective-permute-start | bytes 196616 | tf_op jit(solution)/shard_map/ppermute | solution.py:18
  344.4 11.4 %collective-permute-start.14 = (bf16[1,128,256]{2,1,0:T(8,128)(2,1)}, bf16[1,128,256]{2,1,0:T(8,128)(2,1)S(1)}, u32[]{:S(2)}, u32[]{:S(2)}) collective-permute-start(bf16[1,128,256]{2,1,0:T(8,128)(2,1)} %get-tuple-element.9), channel_id=1, source_target_pairs={{0,1},{1,2},{2,3},{4,5},{5,6},{6,7},{8,9},{9,10},{10,11},{12,13},{... | collective-permute-start | bytes 196616 | tf_op jit(solution)/shard_map/ppermute | solution.py:18
  346.5 9.2 %collective-permute-start.13 = (bf16[1,128,256]{2,1,0:T(8,128)(2,1)}, bf16[1,128,256]{2,1,0:T(8,128)(2,1)S(1)}, u32[]{:S(2)}, u32[]{:S(2)}) collective-permute-start(bf16[1,128,256]{2,1,0:T(8,128)(2,1)} %get-tuple-element.10), channel_id=1, source_target_pairs={{4,0},{8,4},{12,8},{16,12},{20,16},{24,20},{28,24},{5,1},{9,5},{13... | collective-permute-start | bytes 196616 | tf_op jit(solution)/shard_map/ppermute | solution.py:20
  350.5 6.5 %collective-permute-start.15 = (bf16[1,128,256]{2,1,0:T(8,128)(2,1)S(1)}, bf16[1,128,256]{2,1,0:T(8,128)(2,1)}, u32[]{:S(2)}, u32[]{:S(2)}) collective-permute-start(bf16[1,128,256]{2,1,0:T(8,128)(2,1)S(1)} %get-tuple-element.11), channel_id=1, source_target_pairs={{1,0},{2,1},{3,2},{5,4},{6,5},{7,6},{9,8},{10,9},{11,10},{13,12},{... | collective-permute-start | bytes 196616 | tf_op jit(solution)/shard_map/ppermute | solution.py:20
  355.8 0.6 copy-start.5
  356.4 0.6 copy-start.6
Sparse Core Ops, SparseCore 0:
  17.5 96.7 all-gather.4
  198.6 94.9 all-gather.6
